TPU v7x, 256 devices: a whole 4x4x8 slice. The times are simulated.
256 devices in a mesh: member: 16 (over z, x_lo), lat: 8 (over y, core), lon: 2 (over x_hi).
Axes of the slice: x: 4 (x_hi: 2, x_lo: 2; x = x_hi * 2 + x_lo), y: 4, z: 8, core: 2. Of those that a mesh axis runs over, the one named last changes fastest.
Arguments:
- state: bfloat16 [100, 16, 720], P(None, 'lat', 'lon'), may hold values from -6 to 6
- target: bfloat16 [100, 16, 720], P(None, 'lat', 'lon'), may hold values from -6 to 6
- land_sea: int32 [16, 720], P('lat', 'lon'), may hold values 0 or 1
- seeds: int32 [16, 32], P('member'), may hold values from 0 to 65535
- w_in: bfloat16 [9, 100, 256], replicated, may hold values from -0.1875 to 0.1875
- w_mid: bfloat16 [9, 256, 256], replicated, may hold values from -0.125 to 0.125
- w_out: bfloat16 [100, 256], replicated, may hold values from -0.375 to 0.375
- w_noise: float32 [32, 256], replicated, may hold values from -1 to 1
Outputs:
- update_in: float32 [9, 100, 256], replicated
- update_mid: float32 [9, 256, 256], replicated
- update_out: float32 [100, 256], replicated
- update_noise: float32 [32, 256], replicated
- loss: float32 [], replicated
All inputs are finite; a program needn't handle non-finite values. No bound on the sum of `land_sea` on one device may be relied on, other than what follows from the above.
Results may differ from a plain program's by a relative error of at most 0.0014.
Values may be sent and summed in bfloat16 or wider, within the bound.
No kernel may reach another device: no remote copies, remote signals or barrier semaphores. Data moves between devices by JAX's collectives and lax.ppermute only.
A program may use at most 64 MiB of HBM per device.

v0:
```python
import jax
import jax.numpy as jnp
from jax import lax
from jax.sharding import PartitionSpec as P

SMOOTH = 0.25


def with_halo(block, sides, width):
    for axis, dim in sides:
        count = lax.axis_size(axis)
        forward = [(i, i + 1) for i in range(count - 1)]
        forward.append((count - 1, 0))
        backward = [(target, source) for source, target in forward]
        low = lax.ppermute(
            lax.slice_in_dim(block, block.shape[dim] - width, None, axis=dim), axis, forward
        )
        high = lax.ppermute(lax.slice_in_dim(block, 0, width, axis=dim), axis, backward)
        block = jnp.concatenate([low, block, high], axis=dim)
    return block


def shifted(padded, offset, row_count, col_count):
    row_shift = offset // 3
    col_shift = offset % 3
    window = padded[:, row_shift : row_shift + row_count, col_shift : col_shift + col_count]
    return window.reshape(padded.shape[0], row_count * col_count)


def conv_forward(weights, padded, row_count, col_count):
    summed = None
    for offset in range(9):
        window = shifted(padded, offset, row_count, col_count)
        part = lax.dot_general(
            weights[offset], window, (((0,), (0,)), ((), ())), preferred_element_type=jnp.float32
        )
        summed = part if summed is None else summed + part
    return summed


def conv_back(weights, padded, row_count, col_count):
    summed = None
    for offset in range(9):
        window = shifted(padded, 8 - offset, row_count, col_count)
        part = jnp.dot(weights[offset], window, preferred_element_type=jnp.float32)
        summed = part if summed is None else summed + part
    return summed


def weight_grad(padded, deltas, row_count, col_count):
    parts = []
    for offset in range(9):
        window = shifted(padded, offset, row_count, col_count)
        parts.append(
            lax.dot_general(
                window, deltas, (((1,), (1,)), ((), ())), preferred_element_type=jnp.float32
            )
        )
    return jnp.stack(parts)


def gelu_pair(pre):
    return jax.jvp(jax.nn.gelu, (pre,), (jnp.ones_like(pre),))


def clear_outside(padded, width, lat_index, lat_count):
    row_count = padded.shape[1] - 2 * width
    global_row = lat_index * row_count + jnp.arange(padded.shape[1], dtype=jnp.int32) - width
    inside = (global_row >= 0) & (global_row < row_count * lat_count)
    return jnp.where(inside[None, :, None], padded, jnp.zeros((), padded.dtype))


def combine(outputs, target_flat, weights, slope_sum, spread_sum, members):
    misses = outputs - target_flat[None]
    radius = jnp.sqrt(misses * misses + SMOOTH * SMOOTH)
    gradients = weights[None] * (misses / radius / members - slope_sum / (members * (members - 1)))
    loss_term = jnp.sum(
        weights[None] * ((radius - SMOOTH) / members - spread_sum / (2 * members * (members - 1)))
    )
    return (gradients, loss_term)


def pair_sums(outputs, others, running):

    def add_member(totals, member_out):
        gap_value = outputs - member_out.astype(jnp.float32)[None]
        radius = jnp.sqrt(gap_value * gap_value + SMOOTH * SMOOTH)
        return ((totals[0] + gap_value / radius, totals[1] + radius - SMOOTH), None)

    sums, _ = lax.scan(add_member, running, others)
    return sums


def normalize(gradient):
    return gradient / jnp.sqrt(jnp.mean(gradient * gradient) + 1e-06)


def body(state, target, land_sea, seeds, w_in, w_mid, w_out, w_noise):
    variables, row_count, col_count = state.shape
    channels = w_in.shape[2]
    cell_count = row_count * col_count
    lat_index = lax.axis_index("lat")
    lat_count = lax.axis_size("lat")
    members = lax.axis_size("member")
    latent = (seeds[0].astype(jnp.float32) - 32767.5) / 18918.0
    noise_bias = jnp.dot(latent, w_noise, precision=lax.Precision.HIGHEST)
    state_wide = with_halo(state, (("lat", 1), ("lon", 2)), 2)
    state_wide = clear_outside(state_wide, 2, lat_index, lat_count)
    pre_ext = conv_forward(w_in, state_wide, row_count + 2, col_count + 2) + noise_bias[:, None]
    act_ext, slope_ext = gelu_pair(pre_ext)
    hidden_pad = act_ext.astype(jnp.bfloat16).reshape(channels, row_count + 2, col_count + 2)
    hidden_pad = clear_outside(hidden_pad, 1, lat_index, lat_count)
    state_pad = state_wide[:, 1:-1, 1:-1]
    slope_in = slope_ext.reshape(channels, row_count + 2, col_count + 2)[:, 1:-1, 1:-1].reshape(
        channels, cell_count
    )
    hidden_in = hidden_pad[:, 1:-1, 1:-1].reshape(channels, cell_count)
    pre_mid = conv_forward(w_mid, hidden_pad, row_count, col_count)
    act_mid, slope_mid = gelu_pair(pre_mid)
    hidden_out = (act_mid + hidden_in.astype(jnp.float32)).astype(jnp.bfloat16)
    flat_state = state.reshape(variables, cell_count).astype(jnp.float32)
    output = (flat_state + jnp.dot(w_out, hidden_out, preferred_element_type=jnp.float32)).astype(
        jnp.bfloat16
    )
    target_flat = target.reshape(variables, cell_count).astype(jnp.float32)
    weights = 1.0 + land_sea.reshape(1, cell_count).astype(jnp.float32)
    share_cells = cell_count // members
    gathered = lax.all_to_all(output[None], "member", split_axis=2, concat_axis=0, tiled=True)
    first_cell = lax.axis_index("member") * share_cells
    own_target = lax.dynamic_slice_in_dim(target_flat, first_cell, share_cells, 1)
    own_weights = lax.dynamic_slice_in_dim(weights, first_cell, share_cells, 1)
    gathered_f = gathered.astype(jnp.float32)
    blank = jnp.zeros(gathered_f.shape, jnp.float32)
    slope_sum, spread_sum = pair_sums(gathered_f, gathered, (blank, blank))
    gradients, loss_term = combine(
        gathered_f, own_target, own_weights, slope_sum, spread_sum, members
    )
    returned = lax.all_to_all(
        gradients.astype(jnp.bfloat16), "member", split_axis=0, concat_axis=2, tiled=True
    )
    delta_out = returned[0]
    grad_out = lax.dot_general(
        delta_out, hidden_out, (((1,), (1,)), ((), ())), preferred_element_type=jnp.float32
    )
    upstream = lax.dot_general(
        w_out, delta_out, (((0,), (0,)), ((), ())), preferred_element_type=jnp.float32
    )
    delta_mid = (upstream * slope_mid).astype(jnp.bfloat16)
    delta_pad = with_halo(
        delta_mid.reshape(channels, row_count, col_count), (("lat", 1), ("lon", 2)), 1
    )
    delta_pad = clear_outside(delta_pad, 1, lat_index, lat_count)
    incoming = conv_back(w_mid, delta_pad, row_count, col_count) + upstream
    delta_in = (incoming * slope_in).astype(jnp.bfloat16)
    grad_mid = weight_grad(hidden_pad, delta_mid, row_count, col_count)
    grad_in = weight_grad(state_pad, delta_in, row_count, col_count)
    grad_noise = latent[:, None] * jnp.sum(delta_in.astype(jnp.float32), axis=1)[None, :]
    grad_in, grad_mid, grad_out, grad_noise, summed = lax.psum(
        (grad_in, grad_mid, grad_out, grad_noise, loss_term), ("member", "lat", "lon")
    )
    loss = summed / (variables * cell_count * lat_count * lax.axis_size("lon"))
    return (
        normalize(grad_in),
        normalize(grad_mid),
        normalize(grad_out),
        normalize(grad_noise),
        loss,
    )


def solution(mesh):
    placed = (
        P(None, "lat", "lon"),
        P(None, "lat", "lon"),
        P("lat", "lon"),
        P("member", None),
        P(),
        P(),
        P(),
        P(),
    )
    return jax.shard_map(
        body, mesh=mesh, in_specs=placed, out_specs=(P(), P(), P(), P(), P()), check_vma=False
    )
```

profile of v0, /device:TPU:8, one launch (start us, length us, event | category | flops | bytes accessed | tf_op | source)
XLA Modules:
  0.0 410.6 jit_solution(16598785984211095864)
XLA Ops:
  7.2 1.7 collective-permute-start.1
  9.0 0.9 fusion.108
  9.9 2.2 collective-permute-done
  12.1 1.3 pad_maximum_fusion.2
  13.4 3.1 collective-permute-start.2
  17.0 1.0 reshape.240
  18.0 4.2 %collective-permute-done.2 = bf16[100,6,2]{2,1,0:T(8,128)(2,1)S(1)} collective-permute-done((bf16[100,6,2]{2,1,0:T(8,128)(2,1)S(1)}, bf16[100,6,2]{2,1,0:T(8,128)(2,1)S(1)}, u32[]{:S(2)}, u32[]{:S(2)}) %collective-permute-start.2) | collective-permute-done | bytes 2432 | tf_op jit(solution)/shard_map/ppermute | solution.py:15
  22.2 4.4 %collective-permute-done.3 = bf16[100,6,2]{2,1,0:T(8,128)(2,1)S(1)} collective-permute-done((bf16[100,6,2]{2,1,0:T(8,128)(2,1)S(1)}, bf16[100,6,2]{2,1,0:T(8,128)(2,1)S(1)}, u32[]{:S(2)}, u32[]{:S(2)}) %collective-permute-start.3) | collective-permute-done | bytes 2432 | tf_op jit(solution)/shard_map/ppermute | solution.py:18
  26.6 1.3 maximum_select_fusion.1
  27.9 2.1 fusion.116
  31.9 1.3 reshape.207
  33.2 2.0 reshape.208
  35.2 1.3 fusion.97
  39.8 2.4 multiply_convert_fusion
  42.9 0.8 copy-done.2
  45.9 1.3 add_convert_fusion
  47.3 0.7 copy-done.21
  48.3 1.1 copy.20
  49.9 1.9 reduce.2
  51.8 0.9 reshape.246
  52.6 9.5 %all-to-all-start = ((bf16[16,2,2250]{2,1,0:T(2,128)(2,1)}), bf16[16,2,2250]{2,1,0:T(2,128)(2,1)S(1)}, u32[]{:S(2)}, u32[]{:S(2)}) async-start(bf16[16,2,2250]{2,1,0:T(2,128)(2,1)} %reshape.246), calls=%async_computation | async-start | bytes 294912 | tf_op jit(solution)/shard_map/all_to_all | solution.py:128
  62.5 2.7 reshape.229
  65.2 2.0 slice.303
  67.2 5.4 %all-to-all-done = bf16[16,2,2250]{2,1,0:T(2,128)(2,1)S(1)} async-done(((bf16[16,2,2250]{2,1,0:T(2,128)(2,1)}), bf16[16,2,2250]{2,1,0:T(2,128)(2,1)S(1)}, u32[]{:S(2)}, u32[]{:S(2)}) %all-to-all-start) | async-done | bytes 144032 | tf_op jit(solution)/shard_map/all_to_all | solution.py:128
  73.0 1.1 bitcast_reduce_fusion
  74.1 0.8 bitcast_convert_fusion.1
  74.9 1.3 copy.23
  76.2 12.8 %while.15 = (s32[]{:T(128)}, f32[16,100,45]{2,1,0:T(8,128)S(1)}, f32[16,100,45]{2,1,0:T(8,128)S(1)}, bf16[16,100,45]{1,2,0:T(8,128)(2,1)S(1)}, f32[16,100,45]{2,1,0:T(8,128)S(1)}, /*index=5*/s32[]{:T(128)}, s32[]{:T(128)}) while((s32[]{:T(128)}, f32[16,100,45]{2,1,0:T(8,128)S(1)}, f32[16,100,45]{2,1,0:T(8,128)S(1)}, ...), condition=%wide.region_1.2_spmd.clone, body=%wide.region_0.1_spmd.clone.sunk | while | flops 652503 | bytes 1521091 | solution.py:90
  76.4 0.6 fusion.190
  77.2 0.6 fusion.190
  78.0 0.6 fusion.190
  78.8 0.6 fusion.190
  79.6 0.6 fusion.190
  80.4 0.6 fusion.190
  81.2 0.6 fusion.190
  82.0 0.6 fusion.190
  82.8 0.6 fusion.190
  83.6 0.6 fusion.190
  84.4 0.6 fusion.190
  85.2 0.6 fusion.190
  86.8 0.6 fusion.190
  87.6 0.6 fusion.190
  88.4 0.6 fusion.190
  89.7 1.6 multiply_reduce_fusion.2
  91.3 3.5 all-to-all-start.1
  94.9 1.7 fusion.115
  98.1 7.0 %all-to-all-done.1 = bf16[16,100,45]{1,2,0:T(8,128)(2,1)S(1)} async-done(((bf16[16,100,45]{1,2,0:T(8,128)(2,1)}), bf16[16,100,45]{1,2,0:T(8,128)(2,1)S(1)}, u32[]{:S(2)}, u32[]{:S(2)}) %all-to-all-start.1) | async-done | bytes 144032 | tf_op jit(solution)/shard_map/all_to_all | solution.py:138
  106.5 1.7 collective-permute-start.5
  111.5 3.0 collective-permute-start.6
  114.5 0.8 collective-permute-start.7
  115.3 0.9 fusion.118
  116.2 0.7 collective-permute-done.6
  116.9 2.7 collective-permute-done.7
  120.4 0.9 copy-done.3
  123.6 0.8 copy-done.19
  126.8 0.9 copy-done.28
  127.8 75.6 %all-reduce = (f32[32,256]{1,0:T(8,128)S(1)}, f32[]{:T(128)}) all-reduce(f32[32,256]{1,0:T(8,128)S(1)} %broadcast_multiply_fusion, f32[]{:T(128)} %get-tuple-element.162), channel_id=1, replica_groups=mesh['member'=16,'lat'=8,'lon'=2] {'member','lat','lon'}, use_global_device_ids=true, to_apply=%region_9.10 | all-reduce | flops 8193 | bytes 65544 | tf_op jit(solution)/shard_map/psum | solution.py:158
  206.0 185.0 %all-reduce.4.cloned.1.call-done = (f32[9,100,256]{2,1,0:T(8,128)}, f32[9,256,256]{2,1,0:T(8,128)}, f32[100,256]{1,0:T(8,128)}) async-done(((f32[9,100,256]{2,1,0:T(8,128)}, f32[9,256,256]{2,1,0:T(8,128)}, f32[100,256]{1,0:T(8,128)}), (f32[9,100,256]{2,1,0:T(8,128)}, f32[9,256,256]{2,1,0:T(8,128)}, f32[100,256]{1,0:T(8,128)})) %all-reduce.4.cloned.1.call-update) | async-done | bytes 3383312 | tf_op jit(solution)/shard_map/psum | solution.py:158
  390.9 1.7 multiply_reduce_fusion.3
  393.3 1.6 broadcast_divide_fusion.2
  394.9 2.9 multiply_reduce_fusion
  398.5 1.6 broadcast_divide_fusion
  400.1 0.8 multiply_reduce_fusion.1
  401.6 1.0 broadcast_divide_fusion.1
  (208 shorter events, 26.1 us)
Async XLA Ops:
  7.2 40.8 %copy-start = (bf16[100,256]{1,0:T(8,128)(2,1)S(1)}, bf16[100,256]{1,0:T(8,128)(2,1)}, u32[]{:S(2)}) copy-start(bf16[100,256]{1,0:T(8,128)(2,1)} %param.16) | copy-start | bytes 153604
  7.2 19.5 %copy-start.27 = (bf16[100,2,360]{2,1,0:T(2,128)(2,1)S(1)}, bf16[100,2,360]{2,1,0:T(2,128)(2,1)}, u32[]{:S(2)}) copy-start(bf16[100,2,360]{2,1,0:T(2,128)(2,1)} %param.10) | copy-start | bytes 432004
  7.2 4.9 %collective-permute-start = (bf16[100,2,360]{2,1,0:T(2,128)(2,1)}, bf16[100,2,360]{2,1,0:T(2,128)(2,1)S(1)}, u32[]{:S(2)}, u32[]{:S(2)}) collective-permute-start(bf16[100,2,360]{2,1,0:T(2,128)(2,1)} %param.10), channel_id=1, source_target_pairs={{0,2},{2,4},{4,6},{6,8},{8,10},{10,12},{12,14},{14,0},{1,3},{3,5},... | collective-permute-start | bytes 432008 | tf_op jit(solution)/shard_map/ppermute | solution.py:15
  7.2 4.8 %collective-permute-start.1 = (bf16[100,2,360]{2,1,0:T(2,128)(2,1)}, bf16[100,2,360]{2,1,0:T(2,128)(2,1)S(1)}, u32[]{:S(2)}, u32[]{:S(2)}) collective-permute-start(bf16[100,2,360]{2,1,0:T(2,128)(2,1)} %param.10), channel_id=1, source_target_pairs={{2,0},{4,2},{6,4},{8,6},{10,8},{12,10},{14,12},{0,14},{3,1},{5,3},... | collective-permute-start | bytes 432008 | tf_op jit(solution)/shard_map/ppermute | solution.py:18
  13.4 8.9 %collective-permute-start.2 = (bf16[100,6,2]{2,1,0:T(8,128)(2,1)S(1)}, bf16[100,6,2]{2,1,0:T(8,128)(2,1)S(1)}, u32[]{:S(2)}, u32[]{:S(2)}) collective-permute-start(bf16[100,6,2]{2,1,0:T(8,128)(2,1)S(1)} %get-tuple-element.158), channel_id=1, source_target_pairs={{0,1},{1,0},{2,3},{3,2},{4,5},{5,4},{6,7},{7,6},{8,9},{9,8},{10,11... | collective-permute-start | bytes 7208 | tf_op jit(solution)/shard_map/ppermute | solution.py:15
  16.5 10.1 %collective-permute-start.3 = (bf16[100,6,2]{2,1,0:T(8,128)(2,1)S(1)}, bf16[100,6,2]{2,1,0:T(8,128)(2,1)S(1)}, u32[]{:S(2)}, u32[]{:S(2)}) collective-permute-start(bf16[100,6,2]{2,1,0:T(8,128)(2,1)S(1)} %get-tuple-element.159), channel_id=1, source_target_pairs={{1,0},{0,1},{3,2},{2,3},{5,4},{4,5},{7,6},{6,7},{9,8},{8,9},{11,10... | collective-permute-start | bytes 7208 | tf_op jit(solution)/shard_map/ppermute | solution.py:18
  35.2 1.3 copy-start.29
  38.8 1.0 copy-start.30
  42.5 1.3 copy-start.2
  42.8 1.4 copy-start.17
  42.8 1.4 copy-start.23
  42.8 1.4 copy-start.15
  42.8 1.7 copy-start.13
  42.8 2.2 copy-start.9
  42.9 2.5 copy-start.7
  42.9 2.7 copy-start.5
  42.9 3.0 copy-start.11
  42.9 3.0 copy-start.25
  47.3 0.7 copy-start.21
  47.3 14.9 %copy-start.32 = (s32[2,360]{1,0:T(2,128)S(1)}, s32[2,360]{1,0:T(2,128)}, u32[]{:S(2)}) copy-start(s32[2,360]{1,0:T(2,128)} %param.12) | copy-start | bytes 8644
  47.3 14.9 %copy-start.31 = (bf16[100,2,360]{2,1,0:T(2,128)(2,1)S(1)}, bf16[100,2,360]{2,1,0:T(2,128)(2,1)}, u32[]{:S(2)}) copy-start(bf16[100,2,360]{2,1,0:T(2,128)(2,1)} %param.11) | copy-start | bytes 432004
  52.6 20.0 %all-to-all-start = ((bf16[16,2,2250]{2,1,0:T(2,128)(2,1)}), bf16[16,2,2250]{2,1,0:T(2,128)(2,1)S(1)}, u32[]{:S(2)}, u32[]{:S(2)}) async-start(bf16[16,2,2250]{2,1,0:T(2,128)(2,1)} %reshape.246), calls=%async_computation | async-start | bytes 294912 | tf_op jit(solution)/shard_map/all_to_all | solution.py:128
  91.3 13.7 %all-to-all-start.1 = ((bf16[16,100,45]{1,2,0:T(8,128)(2,1)}), bf16[16,100,45]{1,2,0:T(8,128)(2,1)S(1)}, u32[]{:S(2)}, u32[]{:S(2)}) async-start(bf16[16,100,45]{1,2,0:T(8,128)(2,1)} %get-tuple-element.163), calls=%async_computation.1 | async-start | bytes 393216 | tf_op jit(solution)/shard_map/all_to_all | solution.py:138
  94.9 296.1 %all-reduce.4.cloned.1.call-start = ((), (), s32[]{:S(2)}) async-start(), calls=%async_computation.2 | async-start | bytes 6848512 | tf_op jit(solution)/shard_map/psum | solution.py:158
  96.8 8.3 %copy-start.34 = (f32[256,720]{0,1:T(8,128)S(1)}, f32[256,720]{0,1:T(8,128)}, u32[]{:S(2)}) copy-start(f32[256,720]{0,1:T(8,128)} %get-tuple-element.165) | copy-start | bytes 2211844
  105.2 1.0 copy-start.24
  105.7 2.6 copy-start.18
  105.7 2.9 copy-start.16
  106.5 2.5 copy-start.14
  106.5 5.0 %collective-permute-start.4 = (bf16[256,1,360]{0,2,1:T(8,128)(2,1)S(1)}, bf16[256,1,360]{0,2,1:T(8,128)(2,1)S(1)}, u32[]{:S(2)}, u32[]{:S(2)}) collective-permute-start(bf16[256,1,360]{0,2,1:T(8,128)(2,1)S(1)} %get-tuple-element.160), channel_id=1, source_target_pairs={{0,2},{2,4},{4,6},{6,8},{8,10},{10,12},{12,14},{14,0},{1,3},{3,5},... | collective-permute-start | bytes 552968 | tf_op jit(solution)/shard_map/ppermute | solution.py:15
  106.5 2.7 copy-start.12
  106.5 4.9 %collective-permute-start.5 = (bf16[256,1,360]{0,2,1:T(8,128)(2,1)S(1)}, bf16[256,1,360]{0,2,1:T(8,128)(2,1)S(1)}, u32[]{:S(2)}, u32[]{:S(2)}) collective-permute-start(bf16[256,1,360]{0,2,1:T(8,128)(2,1)S(1)} %get-tuple-element.161), channel_id=1, source_target_pairs={{2,0},{4,2},{6,4},{8,6},{10,8},{12,10},{14,12},{0,14},{3,1},{5,3},... | collective-permute-start | bytes 552968 | tf_op jit(solution)/shard_map/ppermute | solution.py:18
  108.6 1.0 copy-start.10
  108.9 1.0 copy-start.8
  109.3 1.0 copy-start.6
  109.6 1.0 copy-start.26
  110.3 5.0 %copy-start.22 = (bf16[256,720]{0,1:T(8,128)(2,1)S(1)}, bf16[256,720]{0,1:T(8,128)(2,1)}, u32[]{:S(2)}) copy-start(bf16[256,720]{0,1:T(8,128)(2,1)} %copy-done.21) | copy-start | bytes 1105924
  111.0 9.4 %copy-start.20 = (f32[9,256,256]{2,1,0:T(8,128)}, f32[9,256,256]{2,1,0:T(8,128)S(1)}, u32[]{:S(2)}) copy-start(f32[9,256,256]{2,1,0:T(8,128)S(1)} %fusion.19) | copy-start | bytes 7077892
  111.5 5.4 %collective-permute-start.6 = (bf16[256,4,1]{0,2,1:T(2,128)(2,1)S(1)}, bf16[256,4,1]{0,2,1:T(2,128)(2,1)S(1)}, u32[]{:S(2)}, u32[]{:S(2)}) collective-permute-start(bf16[256,4,1]{0,2,1:T(2,128)(2,1)S(1)} %get-tuple-element.138), channel_id=1, source_target_pairs={{0,1},{1,0},{2,3},{3,2},{4,5},{5,4},{6,7},{7,6},{8,9},{9,8},{10,11... | collective-permute-start | bytes 6152 | tf_op jit(solution)/shard_map/ppermute | solution.py:15
  114.5 5.1 %collective-permute-start.7 = (bf16[256,4,1]{0,2,1:T(2,128)(2,1)S(1)}, bf16[256,4,1]{0,2,1:T(2,128)(2,1)S(1)}, u32[]{:S(2)}, u32[]{:S(2)}) collective-permute-start(bf16[256,4,1]{0,2,1:T(2,128)(2,1)S(1)} %get-tuple-element.139), channel_id=1, source_target_pairs={{1,0},{0,1},{3,2},{2,3},{5,4},{4,5},{7,6},{6,7},{9,8},{8,9},{11,10... | collective-permute-start | bytes 6152 | tf_op jit(solution)/shard_map/ppermute | solution.py:18
  120.0 1.3 copy-start.3
  123.3 1.1 copy-start.19
  126.8 0.9 copy-start.28
  126.8 1.0 copy-start.33
  390.9 7.5 %copy-start.1 = (f32[9,256,256]{2,1,0:T(8,128)S(1)}, f32[9,256,256]{2,1,0:T(8,128)}, u32[]{:S(2)}) copy-start(f32[9,256,256]{2,1,0:T(8,128)} %get-tuple-element.114) | copy-start | bytes 7077892
  398.5 1.6 copy-start.4
Sparse Core Ops, SparseCore 0:
  127.8 263.0 all-reduce.3
where the time goes:
time: 412 us; the launch traced here: 411 us
  waiting for transfers between devices  212 us (51%)
  blocking collectives  75.6 us (18%)
  local copies, waits for them, and re-layouts  30.9 us (8%)
  other arithmetic  28.4 us (7%)
  starting transfers between devices  24 us (6%)
  matrix products  19.6 us (5%)
  between operations  19.6 us (5%)
    psum x1, waiting for transfers between devices, body(): lax.psum((grad_in, grad_mid, grad_out, grad_noise, loss_term), ('member',...  185 us
    psum x1, blocking collectives, body(): lax.psum((grad_in, grad_mid, grad_out, grad_noise, loss_term), ('member',...  75.6 us
    sub x16, other arithmetic, add_member(): return ((totals[0] + gap_value / radius, totals[1] + radius - SMOOTH), None)  10 us
    dot_general x18, matrix products, conv_forward(): lax.dot_general(weights[offset], window, (((0,), (0,)), ((), ())), prefer...  9.69 us
    all_to_all x1, starting transfers between devices, body(): lax.all_to_all(output[None], 'member', split_axis=2, concat_axis=0, tiled...  9.48 us
    unnamed x74, local copies, waits for them, and re-layouts  8.47 us
  transfers between devices with their start and end apart: 11, of which 9 were waited for; matrix products, arithmetic and copies ran while one was open for 4% of the time, Pallas kernels for 0%

commit v1 on v0

--- a/solution.py
+++ b/solution.py
@@ -156,7 +156,7 @@
     grad_in = weight_grad(state_pad, delta_in, row_count, col_count)
     grad_noise = latent[:, None] * jnp.sum(delta_in.astype(jnp.float32), axis=1)[None, :]
     grad_in, grad_mid, grad_out, grad_noise, summed = lax.psum(
-        (grad_in, grad_mid, grad_out, grad_noise, loss_term), ("member", "lat", "lon")
+        lax.psum((grad_in, grad_mid, grad_out, grad_noise, loss_term), "member"), ("lat", "lon")
     )
     loss = summed / (variables * cell_count * lat_count * lax.axis_size("lon"))
     return (

time: 412 us -> 502 us (1.22)
  blocking collectives: 75.6 us -> 132 us
  waiting for transfers between devices: 212 us -> 243 us
    psum x1 -> x2, blocking collectives: 75.6 us -> 132 us  [the longest x1 66.2 us: body(): lax.psum((grad_in, grad_mid, grad_out, grad_noise, loss_term), 'member')]
    psum x1 -> x2, waiting for transfers between devices: 185 us -> 216 us  [the longest x1 171 us: body(): lax.psum((grad_in, grad_mid, grad_out, grad_noise, loss_term), 'member')]
  transfers between devices with their start and end apart: 11 -> 12, of which waited for: 9 -> 10; matrix products, arithmetic and copies ran while one was open for 4% -> 3% of each run, Pallas kernels for 0% -> 0%
where the time goes in v1:
time: 502 us; the launch traced here: 499 us
  waiting for transfers between devices  243 us (48%)
  blocking collectives  132 us (26%)
  local copies, waits for them, and re-layouts  31.5 us (6%)
  other arithmetic  28.4 us (6%)
  starting transfers between devices  24 us (5%)
  matrix products  19.6 us (4%)
  between operations  19.6 us (4%)
    psum x1, waiting for transfers between devices, body(): lax.psum((grad_in, grad_mid, grad_out, grad_noise, loss_term), 'member')  171 us
    psum x1, blocking collectives, body(): lax.psum((grad_in, grad_mid, grad_out, grad_noise, loss_term), 'member')  66.2 us
    psum x1, blocking collectives, body(): lax.psum(lax.psum((grad_in, grad_mid, grad_out, grad_noise, loss_term), '...  66.1 us
    psum x1, waiting for transfers between devices, body(): lax.psum(lax.psum((grad_in, grad_mid, grad_out, grad_noise, loss_term), '...  45.4 us
  transfers between devices with their start and end apart: 12, of which 10 were waited for; matrix products, arithmetic and copies ran while one was open for 3% of the time, Pallas kernels for 0%

profile of v1, /device:TPU:8, one launch (start us, length us, event | category | flops | bytes accessed | tf_op | source)
XLA Modules:
  0.0 499.2 jit_solution(3338643058337533611)
XLA Ops:
  7.2 1.7 collective-permute-start.1
  9.0 0.9 fusion.108
  9.9 2.2 collective-permute-done
  12.1 1.3 pad_maximum_fusion.2
  13.4 3.1 collective-permute-start.2
  17.0 1.0 reshape.240
  18.0 4.2 collective-permute-done.2
  22.2 4.4 collective-permute-done.3
  26.6 1.3 maximum_select_fusion.1
  27.9 2.1 fusion.116
  31.9 1.3 reshape.207
  33.2 2.0 reshape.208
  35.2 1.3 fusion.97
  39.8 2.4 multiply_convert_fusion
  42.9 0.8 copy-done.2
  45.9 1.3 add_convert_fusion
  47.3 0.7 copy-done.21
  48.3 1.1 copy.20
  49.9 1.9 reduce.2
  51.8 0.9 reshape.246
  52.6 9.5 %all-to-all-start = ((bf16[16,2,2250]{2,1,0:T(2,128)(2,1)}), bf16[16,2,2250]{2,1,0:T(2,128)(2,1)S(1)}, u32[]{:S(2)}, u32[]{:S(2)}) async-start(bf16[16,2,2250]{2,1,0:T(2,128)(2,1)} %reshape.246), calls=%async_computation | async-start | bytes 294912 | tf_op jit(solution)/shard_map/all_to_all | solution.py:128
  62.5 2.7 reshape.229
  65.2 2.0 slice.303
  67.2 5.4 %all-to-all-done = bf16[16,2,2250]{2,1,0:T(2,128)(2,1)S(1)} async-done(((bf16[16,2,2250]{2,1,0:T(2,128)(2,1)}), bf16[16,2,2250]{2,1,0:T(2,128)(2,1)S(1)}, u32[]{:S(2)}, u32[]{:S(2)}) %all-to-all-start) | async-done | bytes 144032 | tf_op jit(solution)/shard_map/all_to_all | solution.py:128
  73.0 1.1 bitcast_reduce_fusion
  74.1 0.8 bitcast_convert_fusion.1
  74.9 1.3 copy.23
  76.2 12.8 %while.15 = (s32[]{:T(128)}, f32[16,100,45]{2,1,0:T(8,128)S(1)}, f32[16,100,45]{2,1,0:T(8,128)S(1)}, bf16[16,100,45]{1,2,0:T(8,128)(2,1)S(1)}, f32[16,100,45]{2,1,0:T(8,128)S(1)}, /*index=5*/s32[]{:T(128)}, s32[]{:T(128)}) while((s32[]{:T(128)}, f32[16,100,45]{2,1,0:T(8,128)S(1)}, f32[16,100,45]{2,1,0:T(8,128)S(1)}, ...), condition=%wide.region_1.2_spmd.clone, body=%wide.region_0.1_spmd.clone.sunk | while | flops 652503 | bytes 1521091 | solution.py:90
  76.4 0.6 fusion.190
  78.0 0.6 fusion.190
  78.8 0.6 fusion.190
  79.6 0.6 fusion.190
  80.4 0.6 fusion.190
  81.2 0.6 fusion.190
  82.0 0.6 fusion.190
  82.8 0.6 fusion.190
  84.4 0.6 fusion.190
  85.2 0.6 fusion.190
  86.8 0.6 fusion.190
  87.6 0.6 fusion.190
  89.7 1.6 multiply_reduce_fusion.2
  91.3 3.5 all-to-all-start.1
  94.9 1.7 fusion.115
  98.1 7.0 %all-to-all-done.1 = bf16[16,100,45]{1,2,0:T(8,128)(2,1)S(1)} async-done(((bf16[16,100,45]{1,2,0:T(8,128)(2,1)}), bf16[16,100,45]{1,2,0:T(8,128)(2,1)S(1)}, u32[]{:S(2)}, u32[]{:S(2)}) %all-to-all-start.1) | async-done | bytes 144032 | tf_op jit(solution)/shard_map/all_to_all | solution.py:138
  106.5 1.7 collective-permute-start.5
  111.5 3.0 collective-permute-start.6
  114.5 0.8 collective-permute-start.7
  115.3 0.9 fusion.118
  116.2 0.7 collective-permute-done.6
  116.9 2.7 collective-permute-done.7
  120.4 0.9 copy-done.3
  123.6 0.8 copy-done.19
  126.8 0.9 copy-done.28
  127.8 170.7 %all-reduce.9.cloned.1.call-done = (f32[9,100,256]{2,1,0:T(8,128)}, f32[9,256,256]{2,1,0:T(8,128)}, f32[100,256]{1,0:T(8,128)}) async-done(((f32[9,100,256]{2,1,0:T(8,128)}, f32[9,256,256]{2,1,0:T(8,128)}, f32[100,256]{1,0:T(8,128)}), (f32[9,100,256]{2,1,0:T(8,128)}, f32[9,256,256]{2,1,0:T(8,128)}, f32[100,256]{1,0:T(8,128)})) %all-reduce.9.cloned.1.call-update) | async-done | bytes 3383312 | tf_op jit(solution)/shard_map/psum | solution.py:159
  298.5 0.6 copy-done.33
  299.2 66.2 %all-reduce.2 = (f32[32,256]{1,0:T(8,128)S(1)}, f32[]{:T(128)}) all-reduce(f32[32,256]{1,0:T(8,128)S(1)} %broadcast_multiply_fusion, f32[]{:T(128)} %get-tuple-element.167), channel_id=1, replica_groups=mesh['member'=16,'lat'=8,'lon'=2] {'member'}, use_global_device_ids=true, to_apply=%region_12.13 | all-reduce | flops 8193 | bytes 65544 | tf_op jit(solution)/shard_map/psum | solution.py:159
  365.4 66.1 %all-reduce = (f32[32,256]{1,0:T(8,128)S(1)}, f32[]{:T(128)}) all-reduce(f32[32,256]{1,0:T(8,128)S(1)} %get-tuple-element.116, f32[]{:T(128)} %get-tuple-element.117), channel_id=1, replica_groups=mesh['member'=16,'lat'=8,'lon'=2] {'lat','lon'}, use_global_device_ids=true, to_apply=%region_13.14 | all-reduce | flops 8193 | bytes 65544 | tf_op jit(solution)/shard_map/psum | solution.py:158
  434.1 45.4 %all-reduce.7.cloned.1.call-done = (f32[9,100,256]{2,1,0:T(8,128)}, f32[9,256,256]{2,1,0:T(8,128)}, f32[100,256]{1,0:T(8,128)}) async-done(((f32[9,100,256]{2,1,0:T(8,128)}, f32[9,256,256]{2,1,0:T(8,128)}, f32[100,256]{1,0:T(8,128)}), (f32[9,100,256]{2,1,0:T(8,128)}, f32[9,256,256]{2,1,0:T(8,128)}, f32[100,256]{1,0:T(8,128)})) %all-reduce.7.cloned.1.call-update) | async-done | bytes 3383312 | tf_op jit(solution)/shard_map/psum | solution.py:158
  479.6 1.7 multiply_reduce_fusion.3
  481.9 1.6 broadcast_divide_fusion.2
  483.5 2.9 multiply_reduce_fusion
  487.1 1.6 broadcast_divide_fusion
  488.7 0.8 multiply_reduce_fusion.1
  490.3 1.0 broadcast_divide_fusion.1
  (212 shorter events, 28.0 us)
Async XLA Ops:
  7.2 40.8 %copy-start = (bf16[100,256]{1,0:T(8,128)(2,1)S(1)}, bf16[100,256]{1,0:T(8,128)(2,1)}, u32[]{:S(2)}) copy-start(bf16[100,256]{1,0:T(8,128)(2,1)} %param.16) | copy-start | bytes 153604
  7.2 19.5 %copy-start.27 = (bf16[100,2,360]{2,1,0:T(2,128)(2,1)S(1)}, bf16[100,2,360]{2,1,0:T(2,128)(2,1)}, u32[]{:S(2)}) copy-start(bf16[100,2,360]{2,1,0:T(2,128)(2,1)} %param.10) | copy-start | bytes 432004
  7.2 4.9 collective-permute-start
  7.2 4.8 collective-permute-start.1
  13.4 8.9 %collective-permute-start.2 = (bf16[100,6,2]{2,1,0:T(8,128)(2,1)S(1)}, bf16[100,6,2]{2,1,0:T(8,128)(2,1)S(1)}, u32[]{:S(2)}, u32[]{:S(2)}) collective-permute-start(bf16[100,6,2]{2,1,0:T(8,128)(2,1)S(1)} %get-tuple-element.163), channel_id=1, source_target_pairs={{0,1},{1,0},{2,3},{3,2},{4,5},{5,4},{6,7},{7,6},{8,9},{9,8},{10,11... | collective-permute-start | bytes 7208 | tf_op jit(solution)/shard_map/ppermute | solution.py:15
  16.5 10.1 %collective-permute-start.3 = (bf16[100,6,2]{2,1,0:T(8,128)(2,1)S(1)}, bf16[100,6,2]{2,1,0:T(8,128)(2,1)S(1)}, u32[]{:S(2)}, u32[]{:S(2)}) collective-permute-start(bf16[100,6,2]{2,1,0:T(8,128)(2,1)S(1)} %get-tuple-element.164), channel_id=1, source_target_pairs={{1,0},{0,1},{3,2},{2,3},{5,4},{4,5},{7,6},{6,7},{9,8},{8,9},{11,10... | collective-permute-start | bytes 7208 | tf_op jit(solution)/shard_map/ppermute | solution.py:18
  35.2 1.3 copy-start.29
  38.8 1.0 copy-start.30
  42.5 1.3 copy-start.2
  42.8 1.4 copy-start.17
  42.8 1.4 copy-start.23
  42.8 1.4 copy-start.15
  42.8 1.7 copy-start.13
  42.8 2.2 copy-start.9
  42.9 2.5 copy-start.7
  42.9 2.7 copy-start.5
  42.9 3.0 copy-start.11
  42.9 3.0 copy-start.25
  47.3 0.7 copy-start.21
  47.3 14.9 %copy-start.32 = (s32[2,360]{1,0:T(2,128)S(1)}, s32[2,360]{1,0:T(2,128)}, u32[]{:S(2)}) copy-start(s32[2,360]{1,0:T(2,128)} %param.12) | copy-start | bytes 8644
  47.3 14.9 %copy-start.31 = (bf16[100,2,360]{2,1,0:T(2,128)(2,1)S(1)}, bf16[100,2,360]{2,1,0:T(2,128)(2,1)}, u32[]{:S(2)}) copy-start(bf16[100,2,360]{2,1,0:T(2,128)(2,1)} %param.11) | copy-start | bytes 432004
  52.6 20.0 %all-to-all-start = ((bf16[16,2,2250]{2,1,0:T(2,128)(2,1)}), bf16[16,2,2250]{2,1,0:T(2,128)(2,1)S(1)}, u32[]{:S(2)}, u32[]{:S(2)}) async-start(bf16[16,2,2250]{2,1,0:T(2,128)(2,1)} %reshape.246), calls=%async_computation | async-start | bytes 294912 | tf_op jit(solution)/shard_map/all_to_all | solution.py:128
  91.3 13.7 %all-to-all-start.1 = ((bf16[16,100,45]{1,2,0:T(8,128)(2,1)}), bf16[16,100,45]{1,2,0:T(8,128)(2,1)S(1)}, u32[]{:S(2)}, u32[]{:S(2)}) async-start(bf16[16,100,45]{1,2,0:T(8,128)(2,1)} %get-tuple-element.168), calls=%async_computation.1 | async-start | bytes 393216 | tf_op jit(solution)/shard_map/all_to_all | solution.py:138
  94.9 203.6 %all-reduce.9.cloned.1.call-start = ((), (), s32[]{:S(2)}) async-start(), calls=%async_computation.3 | async-start | bytes 6848512 | tf_op jit(solution)/shard_map/psum | solution.py:159
  96.8 8.3 %copy-start.34 = (f32[256,720]{0,1:T(8,128)S(1)}, f32[256,720]{0,1:T(8,128)}, u32[]{:S(2)}) copy-start(f32[256,720]{0,1:T(8,128)} %get-tuple-element.170) | copy-start | bytes 2211844
  105.2 1.0 copy-start.24
  105.7 2.6 copy-start.18
  105.7 2.9 copy-start.16
  106.5 2.5 copy-start.14
  106.5 5.0 collective-permute-start.4
  106.5 2.7 copy-start.12
  106.5 4.9 collective-permute-start.5
  108.6 1.0 copy-start.10
  108.9 1.0 copy-start.8
  109.3 1.0 copy-start.6
  109.6 1.0 copy-start.26
  110.3 5.0 %copy-start.22 = (bf16[256,720]{0,1:T(8,128)(2,1)S(1)}, bf16[256,720]{0,1:T(8,128)(2,1)}, u32[]{:S(2)}) copy-start(bf16[256,720]{0,1:T(8,128)(2,1)} %copy-done.21) | copy-start | bytes 1105924
  111.0 9.4 %copy-start.20 = (f32[9,256,256]{2,1,0:T(8,128)}, f32[9,256,256]{2,1,0:T(8,128)S(1)}, u32[]{:S(2)}) copy-start(f32[9,256,256]{2,1,0:T(8,128)S(1)} %fusion.19) | copy-start | bytes 7077892
  111.5 5.4 %collective-permute-start.6 = (bf16[256,4,1]{0,2,1:T(2,128)(2,1)S(1)}, bf16[256,4,1]{0,2,1:T(2,128)(2,1)S(1)}, u32[]{:S(2)}, u32[]{:S(2)}) collective-permute-start(bf16[256,4,1]{0,2,1:T(2,128)(2,1)S(1)} %get-tuple-element.143), channel_id=1, source_target_pairs={{0,1},{1,0},{2,3},{3,2},{4,5},{5,4},{6,7},{7,6},{8,9},{9,8},{10,11... | collective-permute-start | bytes 6152 | tf_op jit(solution)/shard_map/ppermute | solution.py:15
  114.5 5.1 %collective-permute-start.7 = (bf16[256,4,1]{0,2,1:T(2,128)(2,1)S(1)}, bf16[256,4,1]{0,2,1:T(2,128)(2,1)S(1)}, u32[]{:S(2)}, u32[]{:S(2)}) collective-permute-start(bf16[256,4,1]{0,2,1:T(2,128)(2,1)S(1)} %get-tuple-element.144), channel_id=1, source_target_pairs={{1,0},{0,1},{3,2},{2,3},{5,4},{4,5},{7,6},{6,7},{9,8},{8,9},{11,10... | collective-permute-start | bytes 6152 | tf_op jit(solution)/shard_map/ppermute | solution.py:18
  120.0 1.3 copy-start.3
  123.3 1.1 copy-start.19
  126.8 0.9 copy-start.28
  127.7 351.8 %all-reduce.7.cloned.1.call-start = ((), (), s32[]{:S(2)}) async-start(), calls=%async_computation.2 | async-start | bytes 6848512 | tf_op jit(solution)/shard_map/psum | solution.py:158
  298.5 0.7 copy-start.33
  479.6 7.5 %copy-start.1 = (f32[9,256,256]{2,1,0:T(8,128)S(1)}, f32[9,256,256]{2,1,0:T(8,128)}, u32[]{:S(2)}) copy-start(f32[9,256,256]{2,1,0:T(8,128)} %get-tuple-element.114) | copy-start | bytes 7077892
  487.1 1.6 copy-start.4
Sparse Core Ops, SparseCore 0:
  127.8 170.6 all-reduce.8
  301.4 178.1 all-reduce.6
